TPU v7x, 128 devices: a whole 4x4x4 slice. The times are simulated.
128 devices in a mesh: req: 32 (over x, z, core), tp: 4 (over y).
Axes of the slice: x: 4, y: 4, z: 4, core: 2. Of those that a mesh axis runs over, the one named last changes fastest.
Arguments:
- tokens: bfloat16 [1024, 2048], P('req'), may hold values from -6 to 6
- deal_order: int32 [1024], replicated, may hold values from 0 to 1023, as said below
- page_table: int32 [1024, 6], P('req'), may hold values from 0 to 1343, as said below
- lengths: int32 [1024], P('req'), may hold values from 1 to 768, as said below
- qkv_weight: bfloat16 [2048, 3, 2048], P(None, None, 'tp'), may hold values from -0.125 to 0.125
- out_weight: bfloat16 [2048, 2048], P('tp'), may hold values from -0.125 to 0.125
- up_weight: bfloat16 [2048, 4096], P(None, 'tp'), may hold values from -0.125 to 0.125
- down_weight: bfloat16 [4096, 2048], P('tp'), may hold values from -0.09375 to 0.09375
- key_cache: bfloat16 [2, 1344, 128, 2048], P(None, 'req', None, 'tp')
- value_cache: bfloat16 [2, 1344, 128, 2048], P(None, 'req', None, 'tp'), may hold values from -6 to 6
- attn_norm: float32 [2, 2048], replicated
- mlp_norm: float32 [2, 2048], replicated
Outputs:
- output: bfloat16 [1024, 2048], P('req')
Inputs may be any that keep to these rules, and one draw needn't show every extreme that they name: `deal_order`: A permutation: every request is placed in exactly one slot. Of the 32 requests in the slots s // 32 = d of one block d, at most 2 come from one source block of rows r // 32 = j, and some pair of blocks has exactly 2. `page_table`: row s holds the pages of the request in dealt slot s: its first ceil(lengths[s] / 128) entries are pages of the block s // 32 * 42 to s // 32 * 42 + 41, no page serves two slots, and the remaining entries repeat the row's first page. `lengths`: A request fills at most 6 pages; the slots s // 32 = d of one block d fill at most 42 pages together, and some block fills exactly that many.
All inputs are finite; a program needn't handle non-finite values.
Results may differ from a plain program's by a relative error of at most 0.034.
Values may be sent and summed in bfloat16 or wider, within the bound.
No kernel may reach another device: no remote copies, remote signals or barrier semaphores. Data moves between devices by JAX's collectives and lax.ppermute only.
A program may use at most 448 MiB of HBM per device.

v0:
```python
import math
import jax
import jax.numpy as jnp
from jax import lax
from jax.sharding import PartitionSpec as P

HD = 128
epsilon = 1e-06


def layer_norm(row_total, gain_bias):
    row_mean = jnp.mean(row_total, axis=-1, keepdims=True)
    centered = row_total - row_mean
    row_var = jnp.mean(centered * centered, axis=-1, keepdims=True)
    return (centered * lax.rsqrt(row_var + epsilon) * gain_bias[0] + gain_bias[1]).astype(
        jnp.bfloat16
    )


def post_norm(partial_term, residual, gain_bias):
    row_total = lax.psum(partial_term.astype(jnp.bfloat16), "tp").astype(
        jnp.float32
    ) + residual.astype(jnp.float32)
    return layer_norm(row_total, gain_bias)


def head_masks(feat_share, head_dim):
    head_count = feat_share // head_dim
    owner = jnp.arange(feat_share, dtype=jnp.int32) // head_dim
    return owner[None, :] == jnp.arange(head_count, dtype=jnp.int32)[:, None]


def spread_query(query_flat, mask):
    return jnp.where(mask[None, :, :], query_flat[:, None, :], jnp.zeros((), query_flat.dtype))


def own_scores(query_flat, key_new, mask, score_scale):
    product = query_flat.astype(jnp.float32) * key_new.astype(jnp.float32)
    return jnp.sum(jnp.where(mask[None, :, :], product[:, None, :], 0.0), axis=-1) * score_scale


def finish_mix(scores, own_score, value_new, mask, mix_fn):
    row_max = jnp.maximum(jnp.max(scores, axis=-1), own_score)
    exp_cache = jnp.exp(scores - row_max[..., None])
    exp_own = jnp.exp(own_score - row_max)
    row_total = jnp.sum(exp_cache, axis=-1) + exp_own
    cache_weights = (exp_cache / row_total[..., None]).astype(jnp.bfloat16)
    own_weight = (exp_own / row_total).astype(jnp.bfloat16).astype(jnp.float32)
    mixed_wide = mix_fn(cache_weights)
    mixed_cache = jnp.sum(jnp.where(mask[None, :, :], mixed_wide, 0.0), axis=1)
    own_spread = jnp.sum(jnp.where(mask[None, :, :], own_weight[:, :, None], 0.0), axis=1)
    return mixed_cache + own_spread * value_new.astype(jnp.float32)


def attend_pool(
    query_flat, key_new, value_new, key_pool, value_pool, local_table, lengths, score_scale, mask
):
    req_rows, feat_share = query_flat.shape
    pool_pages, page_len = (key_pool.shape[0], key_pool.shape[1])
    slot_count = local_table.shape[1]
    page_ids = jnp.arange(pool_pages, dtype=jnp.int32)
    slot_ids = jnp.arange(slot_count, dtype=jnp.int32)
    slot_used = slot_ids[None, :] * page_len < lengths[:, None]
    page_hit = (local_table[:, :, None] == page_ids[None, None, :]) & slot_used[:, :, None]
    start_pos = jnp.sum(jnp.where(page_hit, slot_ids[None, :, None] * page_len, 0), axis=1)
    is_owned = jnp.any(page_hit, axis=1)
    position = start_pos[:, :, None] + jnp.arange(page_len, dtype=jnp.int32)[None, None, :]
    is_valid = (is_owned[:, :, None] & (position < lengths[:, None, None])).reshape(
        req_rows, pool_pages * page_len
    )
    flat_keys = key_pool.reshape(pool_pages * page_len, feat_share)
    flat_values = value_pool.reshape(pool_pages * page_len, feat_share)
    query_wide = spread_query(query_flat, mask)
    scores = (
        jnp.einsum("rhf,tf->rht", query_wide, flat_keys, preferred_element_type=jnp.float32)
        * score_scale
    )
    scores = jnp.where(is_valid[:, None, :], scores, -jnp.inf)
    own_score = own_scores(query_flat, key_new, mask, score_scale)

    def mix_pool(cache_weights):
        return jnp.einsum(
            "rht,tf->rhf", cache_weights, flat_values, preferred_element_type=jnp.float32
        )

    return finish_mix(scores, own_score, value_new, mask, mix_pool)


def local(
    tokens,
    deal_order,
    page_table,
    lengths,
    qkv_weight,
    out_weight,
    up_weight,
    down_weight,
    key_cache,
    value_cache,
    attn_norm,
    mlp_norm,
):
    req_rows, model_width = tokens.shape
    tp_count = lax.axis_size("tp")
    req_index = lax.axis_index("req")
    feat_share = model_width // tp_count
    score_scale = 1.0 / math.sqrt(HD)
    mask = head_masks(feat_share, HD)
    dealt_here = lax.dynamic_slice_in_dim(deal_order, req_index * req_rows, req_rows)
    everyone = lax.all_gather(tokens, "req", axis=0, tiled=True)
    current = jnp.take(everyone, dealt_here, axis=0)
    pool_pages = key_cache.shape[1]
    local_table = page_table - req_index * pool_pages
    qkv_flat = qkv_weight.reshape(model_width, 3 * feat_share)
    for layer_index in range(key_cache.shape[0]):
        projected = jnp.dot(current, qkv_flat, preferred_element_type=jnp.float32).astype(
            jnp.bfloat16
        )
        query_flat = projected[:, :feat_share]
        key_new = projected[:, feat_share : 2 * feat_share]
        value_new = projected[:, 2 * feat_share :]
        key_pool = key_cache[layer_index]
        value_pool = value_cache[layer_index]
        attended = attend_pool(
            query_flat,
            key_new,
            value_new,
            key_pool,
            value_pool,
            local_table,
            lengths,
            score_scale,
            mask,
        )
        attended = attended.astype(jnp.bfloat16)
        attn_term = jnp.dot(attended, out_weight, preferred_element_type=jnp.float32)
        hidden = post_norm(attn_term, current, attn_norm)
        up_proj = jnp.dot(hidden, up_weight, preferred_element_type=jnp.float32)
        activated = jax.nn.gelu(up_proj, approximate=True).astype(jnp.bfloat16)
        down_term = jnp.dot(activated, down_weight, preferred_element_type=jnp.float32)
        current = post_norm(down_term, hidden, mlp_norm)
    request_count = deal_order.shape[0]
    inverse = (
        jnp.zeros_like(deal_order).at[deal_order].set(jnp.arange(request_count, dtype=jnp.int32))
    )
    inverse_here = lax.dynamic_slice_in_dim(inverse, req_index * req_rows, req_rows)
    returned = lax.all_gather(current, "req", axis=0, tiled=True)
    result = jnp.take(returned, inverse_here, axis=0)
    return result


def solution(mesh):
    in_specs = (
        P("req", None),
        P(),
        P("req", None),
        P("req"),
        P(None, None, "tp"),
        P("tp", None),
        P(None, "tp"),
        P("tp", None),
        P(None, "req", None, "tp"),
        P(None, "req", None, "tp"),
        P(),
        P(),
    )
    out_specs = P("req", None)
    return jax.shard_map(local, mesh=mesh, in_specs=in_specs, out_specs=out_specs, check_vma=False)
```

profile of v0, /device:TPU:1, one launch (start us, length us, event | category | flops | bytes accessed | tf_op | source)
XLA Modules:
  0.0 334.8 jit_solution(1223456797249646341)
XLA Ops:
  7.3 8.8 %copy.16 = bf16[2048,3,512]{0,2,1:T(8,128)(2,1)} copy(bf16[2048,3,512]{2,0,1:T(8,128)(2,1)} %param.18) | data formatting | bytes 12582912 | tf_op args[4]
  16.7 9.8 %fusion.77 = (bf16[1,42,128,512]{3,2,1,0:T(8,128)(2,1)}, bf16[1,42,128,512]{3,2,1,0:T(8,128)(2,1)}) fusion(bf16[2,42,128,512]{3,2,1,0:T(8,128)(2,1)} %param.22), kind=kLoop, calls=%fused_computation.147 | loop fusion | bytes 22020096 | tf_op jit(solution)/shard_map/slice | solution.py:122
  26.4 9.7 %fusion.78 = (bf16[1,42,128,512]{3,2,1,0:T(8,128)(2,1)}, bf16[1,42,128,512]{3,2,1,0:T(8,128)(2,1)}) fusion(bf16[2,42,128,512]{3,2,1,0:T(8,128)(2,1)} %param.23), kind=kLoop, calls=%fused_computation.148 | loop fusion | bytes 22020096 | tf_op jit(solution)/shard_map/slice | solution.py:123
  37.0 22.6 %all-gather.3.cloned.1.call-done = bf16[1024,2048]{1,0:T(8,128)(2,1)} async-done(((bf16[32,2048]{1,0:T(8,128)(2,1)}), bf16[1024,2048]{1,0:T(8,128)(2,1)}) %all-gather.3.cloned.1.call-update) | async-done | bytes 4194320 | tf_op jit(solution)/shard_map/all_gather | solution.py:110
  59.7 3.5 %gather_fusion = bf16[32,2048]{1,0:T(8,128)(2,1)S(1)} fusion(bf16[1024,2048]{1,0:T(8,128)(2,1)} %all-gather.3.cloned.1.call-done, s32[1024]{0:T(1024)S(1)} %pad_clamp_fusion.1), kind=kCustom, calls=%fused_computation.clone | custom fusion | bytes 262272 | tf_op jit(solution)/shard_map/jit(_take)/gather | solution.py:111
  63.2 4.9 %convolution_convert_fusion.1 = bf16[32,1536]{1,0:T(8,128)(2,1)S(1)} fusion(bf16[2048,1536]{0,1:T(8,128)(2,1)} %bitcast.44, bf16[32,2048]{1,0:T(8,128)(2,1)S(1)} %gather_fusion, pred[32]{0:T(512)(128)(4,1)S(1)} %get-tuple-element.8), kind=kOutput, calls=%fused_computation.14 | convolution fusion | flops 201441280 | bytes 6520864 | tf_op jit(solution)/shard_map/dot_general | solution.py:116
  68.3 2.0 fusion.81
  71.0 1.0 fusion.8
  72.1 1.1 convolution_convert_fusion.5
  73.3 38.0 %all-reduce.5.cloned.1.call-done = bf16[32,2048]{1,0:T(8,128)(2,1)} async-done(((bf16[32,2048]{1,0:T(8,128)(2,1)}), bf16[32,2048]{1,0:T(8,128)(2,1)}) %all-reduce.5.cloned.1.call-update) | async-done | bytes 131088 | tf_op jit(solution)/shard_map/psum | solution.py:21
  111.3 1.1 fusion.13
  112.5 1.1 multiply_reduce_fusion.3
  113.6 1.1 add_convert_fusion.3
  114.7 5.7 %convolution_convert_fusion.4 = bf16[32,2048]{1,0:T(8,128)(2,1)} fusion(bf16[1024,2048]{1,0:T(8,128)(2,1)} %param.21, bf16[32,2048]{1,0:T(8,128)(2,1)S(1)} %add_convert_fusion.3, bf16[2048,1024]{1,0:T(8,128)(2,1)} %param.20), kind=kOutput, calls=%fused_computation.17 | convolution fusion | flops 268795904 | bytes 8650752 | tf_op jit(solution)/shard_map/dot_general | solution.py:140
  120.7 41.5 %all-reduce.7.cloned.1.call-done = bf16[32,2048]{1,0:T(8,128)(2,1)} async-done(((bf16[32,2048]{1,0:T(8,128)(2,1)}), bf16[32,2048]{1,0:T(8,128)(2,1)}) %all-reduce.7.cloned.1.call-update) | async-done | bytes 131088 | tf_op jit(solution)/shard_map/psum | solution.py:21
  162.2 1.0 fusion.15
  163.3 1.1 multiply_reduce_fusion.2
  165.4 4.9 %convolution_convert_fusion = bf16[32,1536]{1,0:T(8,128)(2,1)S(1)} fusion(bf16[32,2048]{1,0:T(8,128)(2,1)S(1)} %add_convert_fusion.2, bf16[2048,1536]{0,1:T(8,128)(2,1)} %bitcast.45), kind=kOutput, calls=%fused_computation.13 | convolution fusion | flops 201375744 | bytes 6520832 | tf_op jit(solution)/shard_map/dot_general | solution.py:116
  170.5 4.7 %fusion.82 = (f32[32,4]{0,1:T(4,128)S(1)}, f32[32,4,5376]{2,0,1:T(8,128)S(1)}) fusion(bf16[5376,512,1]{1,0,2:T(8,128)(2,1)} %bitcast.46, pred[4,512]{1,0:T(4,128)(4,1)S(1)} %iota_compare_fusion.1, bf16[32,512]{1,0:T(8,128)(2,1)S(1)} %slice.67, pred[32,5376]{1,0:T(8,128)(4,1)S(1)} %fusion.11), kind=kOutput, calls=%fused_computation.152 | convolution fusion | flops 706772864 | bytes 8464896 | tf_op jit(solution)/shard_map/rhf,tf->rht/dot_general | solution.py:75
  175.8 1.0 fusion.9
  176.9 1.1 convolution_convert_fusion.3
  178.1 41.7 %all-reduce.9.cloned.1.call-done = bf16[32,2048]{1,0:T(8,128)(2,1)} async-done(((bf16[32,2048]{1,0:T(8,128)(2,1)}), bf16[32,2048]{1,0:T(8,128)(2,1)}) %all-reduce.9.cloned.1.call-update) | async-done | bytes 131088 | tf_op jit(solution)/shard_map/psum | solution.py:21
  219.7 1.0 fusion.17
  220.8 1.1 multiply_reduce_fusion.1
  222.9 5.7 %convolution_convert_fusion.2 = bf16[32,2048]{1,0:T(8,128)(2,1)} fusion(bf16[1024,2048]{1,0:T(8,128)(2,1)} %param.21, bf16[32,2048]{1,0:T(8,128)(2,1)S(1)} %add_convert_fusion.1, bf16[2048,1024]{1,0:T(8,128)(2,1)} %param.20), kind=kOutput, calls=%fused_computation.15 | convolution fusion | flops 268795904 | bytes 8650752 | tf_op jit(solution)/shard_map/dot_general | solution.py:140
  228.7 41.7 %all-reduce.11.cloned.1.call-done = bf16[32,2048]{1,0:T(8,128)(2,1)} async-done(((bf16[32,2048]{1,0:T(8,128)(2,1)}), bf16[32,2048]{1,0:T(8,128)(2,1)}) %all-reduce.11.cloned.1.call-update) | async-done | bytes 131088 | tf_op jit(solution)/shard_map/psum | solution.py:21
  270.4 1.0 fusion.19
  271.5 1.1 multiply_reduce_fusion
  272.6 1.7 add_convert_fusion
  274.3 4.3 %scatter_custom_fusion = s32[1024]{0:T(1024)S(1)} fusion(s32[1024]{0:T(1024)S(1)} %compare_select_fusion, s32[1024]{0:T(1024)S(1)} %iota.51, s32[]{:T(128)} %constant.32.clone.1), kind=kCustom, calls=%fused_computation.111 | custom fusion | bytes 4100 | tf_op jit(solution)/shard_map/scatter | solution.py:144
  278.7 45.0 %all-gather.5.cloned.1.call-done = bf16[1024,2048]{1,0:T(8,128)(2,1)} async-done(((bf16[32,2048]{1,0:T(8,128)(2,1)}), bf16[1024,2048]{1,0:T(8,128)(2,1)}) %all-gather.5.cloned.1.call-update) | async-done | bytes 4194320 | tf_op jit(solution)/shard_map/all_gather | solution.py:147
  323.7 3.5 %gather_fusion.1 = bf16[32,2048]{1,0:T(8,128)(2,1)S(1)} fusion(bf16[1024,2048]{1,0:T(8,128)(2,1)} %all-gather.5.cloned.1.call-done, s32[1024]{0:T(1024)S(1)} %pad_clamp_fusion), kind=kCustom, calls=%fused_computation.1.clone | custom fusion | bytes 262272 | tf_op jit(solution)/shard_map/jit(_take)/gather | solution.py:148
  (80 shorter events, 7.1 us)
Async XLA Ops:
  6.5 65.5 %copy-start = (bf16[512,2048]{1,0:T(8,128)(2,1)S(1)}, bf16[512,2048]{1,0:T(8,128)(2,1)}, u32[]{:S(2)}) copy-start(bf16[512,2048]{1,0:T(8,128)(2,1)} %param.19) | copy-start | bytes 6291460
  6.5 53.1 %all-gather.3.cloned.1.call-start = ((), (), s32[]{:S(2)}) async-start(), calls=%async_computation | async-start | bytes 4325376 | tf_op jit(solution)/shard_map/all_gather | solution.py:110
  7.3 104.1 %all-reduce.5.cloned.1.call-start = ((), (), s32[]{:S(2)}) async-start(), calls=%async_computation.1 | async-start | bytes 262144 | tf_op jit(solution)/shard_map/psum | solution.py:21
  7.3 8.9 %copy-start.4 = (s32[1024]{0:T(1024)S(1)}, s32[1024]{0:T(1024)}, u32[]{:S(2)}) copy-start(s32[1024]{0:T(1024)} %param.15) | copy-start | bytes 12292
  7.3 9.0 %copy-start.6 = (s32[32]{0:T(128)S(1)}, s32[32]{0:T(128)}, u32[]{:S(2)}) copy-start(s32[32]{0:T(128)} %param.17) | copy-start | bytes 388
  7.3 9.1 %copy-start.5 = (s32[32,6]{0,1:T(8,128)S(1)}, s32[32,6]{0,1:T(8,128)}, u32[]{:S(2)}) copy-start(s32[32,6]{0,1:T(8,128)} %param.16) | copy-start | bytes 2308
  63.2 5.1 %copy-start.1 = (bf16[1,42,128,512]{3,2,1,0:T(8,128)(2,1)S(1)}, bf16[1,42,128,512]{3,2,1,0:T(8,128)(2,1)}, u32[]{:S(2)}) copy-start(bf16[1,42,128,512]{3,2,1,0:T(8,128)(2,1)} %get-tuple-element.11) | copy-start | bytes 16515076
  68.1 2.9 slice-start.2
  68.3 2.7 slice-start.3
  71.0 2.3 copy-start.2
  73.2 89.0 %all-reduce.7.cloned.1.call-start = ((), (), s32[]{:S(2)}) async-start(), calls=%async_computation.2 | async-start | bytes 262144 | tf_op jit(solution)/shard_map/psum | solution.py:21
  114.7 6.0 %copy-start.3 = (f32[2,2048]{1,0:T(2,128)S(1)}, f32[2,2048]{1,0:T(2,128)}, u32[]{:S(2)}) copy-start(f32[2,2048]{1,0:T(2,128)} %param.25) | copy-start | bytes 49156
  120.5 99.3 %all-reduce.9.cloned.1.call-start = ((), (), s32[]{:S(2)}) async-start(), calls=%async_computation.3 | async-start | bytes 262144 | tf_op jit(solution)/shard_map/psum | solution.py:21
  165.4 10.4 %slice-start = ((s8[5505024]{0:T(1024)(128)(4,1)}), s8[4194304]{0:T(1024)(128)(4,1)S(1)}, s32[]{:S(2)}) async-start(s8[5505024]{0:T(1024)(128)(4,1)} %bitcast.48), calls=%async_computation.6 | async-start | bytes 8388608
  170.5 5.4 %slice-start.1 = ((s8[5505024]{0:T(1024)(128)(4,1)}), s8[1310720]{0:T(1024)(128)(4,1)S(1)}, s32[]{:S(2)}) async-start(s8[5505024]{0:T(1024)(128)(4,1)} %bitcast.48), calls=%async_computation.7 | async-start | bytes 2621440
  178.0 92.4 %all-reduce.11.cloned.1.call-start = ((), (), s32[]{:S(2)}) async-start(), calls=%async_computation.4 | async-start | bytes 262144 | tf_op jit(solution)/shard_map/psum | solution.py:21
  228.7 95.1 %all-gather.5.cloned.1.call-start = ((), (), s32[]{:S(2)}) async-start(), calls=%async_computation.5 | async-start | bytes 4325376 | tf_op jit(solution)/shard_map/all_gather | solution.py:147
Sparse Core Ops, SparseCore 0:
  9.6 50.0 all-gather.2
  73.3 37.9 all-reduce.4
  120.6 41.5 all-reduce.6
  178.1 41.5 all-reduce.8
  228.8 41.5 all-reduce.10
  274.4 49.2 all-gather.4
where the time goes:
time: 335 us
  waiting for transfers between devices  231 us (69%)
  local copies, waits for them, and re-layouts  40.3 us (12%)
  matrix products  32.2 us (10%)
  other arithmetic  16.7 us (5%)
  between operations  13.9 us (4%)
    psum x4, waiting for transfers between devices, post_norm(): lax.psum(partial_term.astype(jnp.bfloat16), 'tp').astype(jnp.float32)  163 us
    all_gather x1, waiting for transfers between devices, local(): returned = lax.all_gather(current, 'req', axis=0, tiled=True)  45 us
    all_gather x1, waiting for transfers between devices, local(): everyone = lax.all_gather(tokens, 'req', axis=0, tiled=True)  22.6 us
    dot_general x2, matrix products, local(): jnp.dot(activated, down_weight, preferred_element_type=jnp.float32)  11.4 us
    dot_general x2, matrix products, local(): jnp.dot(current, qkv_flat, preferred_element_type=jnp.float32)  9.8 us
    slice x1, local copies, waits for them, and re-layouts, local(): key_pool = key_cache[layer_index]  9.76 us
    slice x1, local copies, waits for them, and re-layouts, local(): value_pool = value_cache[layer_index]  9.75 us
    unnamed x23, local copies, waits for them, and re-layouts  8.92 us
  transfers between devices with their start and end apart: 6, of which 6 were waited for; matrix products, arithmetic and copies ran while one was open for 10% of the time, Pallas kernels for 0%

commit v1 on v0

--- a/solution.py
+++ b/solution.py
@@ -144,7 +144,9 @@
         jnp.zeros_like(deal_order).at[deal_order].set(jnp.arange(request_count, dtype=jnp.int32))
     )
     inverse_here = lax.dynamic_slice_in_dim(inverse, req_index * req_rows, req_rows)
-    returned = lax.all_gather(current, "req", axis=0, tiled=True)
+    returned = jnp.concatenate(
+        lax.all_to_all(jnp.stack([current] * lax.axis_size("req")), "req", 0, 0), axis=0
+    )
     result = jnp.take(returned, inverse_here, axis=0)
     return result
 

time: 335 us -> 350 us (1.045)
  starting transfers between devices: 0.39 us -> 10.1 us
    all_to_all x0 -> x1, waiting for transfers between devices: none -> 47.8 us  [local(): lax.all_to_all(jnp.stack([current] * lax.axis_size('req')), 'req', 0, 0)]
    all_gather x1 -> x0, waiting for transfers between devices: 45 us -> none  [local(): returned = lax.all_gather(current, 'req', axis=0, tiled=True)]
    all_to_all x0 -> x1, starting transfers between devices: none -> 9.79 us  [local(): lax.all_to_all(jnp.stack([current] * lax.axis_size('req')), 'req', 0, 0)]
where the time goes in v1:
time: 350 us; the launch traced here: 349 us
  waiting for transfers between devices  234 us (67%)
  local copies, waits for them, and re-layouts  42.8 us (12%)
  matrix products  32.2 us (9%)
  other arithmetic  16.1 us (5%)
  between operations  13.6 us (4%)
  starting transfers between devices  10.1 us (3%)
    psum x4, waiting for transfers between devices, post_norm(): lax.psum(partial_term.astype(jnp.bfloat16), 'tp').astype(jnp.float32)  163 us
    all_to_all x1, waiting for transfers between devices, local(): lax.all_to_all(jnp.stack([current] * lax.axis_size('req')), 'req', 0, 0)  47.8 us
    all_gather x1, waiting for transfers between devices, local(): everyone = lax.all_gather(tokens, 'req', axis=0, tiled=True)  22.6 us
    dot_general x2, matrix products, local(): jnp.dot(activated, down_weight, preferred_element_type=jnp.float32)  11.4 us
    dot_general x2, matrix products, local(): jnp.dot(current, qkv_flat, preferred_element_type=jnp.float32)  9.8 us
    all_to_all x1, starting transfers between devices, local(): lax.all_to_all(jnp.stack([current] * lax.axis_size('req')), 'req', 0, 0)  9.79 us
    slice x1, local copies, waits for them, and re-layouts, local(): key_pool = key_cache[layer_index]  9.76 us
    slice x1, local copies, waits for them, and re-layouts, local(): value_pool = value_cache[layer_index]  9.75 us
  transfers between devices with their start and end apart: 6, of which 6 were waited for; matrix products, arithmetic and copies ran while one was open for 10% of the time, Pallas kernels for 0%

profile of v1, /device:TPU:1, one launch (start us, length us, event | category | flops | bytes accessed | tf_op | source)
XLA Modules:
  0.0 348.9 jit_solution(10504656967697662062)
XLA Ops:
  7.3 8.8 %copy.16 = bf16[2048,3,512]{0,2,1:T(8,128)(2,1)} copy(bf16[2048,3,512]{2,0,1:T(8,128)(2,1)} %param.18) | data formatting | bytes 12582912 | tf_op args[4]
  16.7 9.8 %fusion.77 = (bf16[1,42,128,512]{3,2,1,0:T(8,128)(2,1)}, bf16[1,42,128,512]{3,2,1,0:T(8,128)(2,1)}) fusion(bf16[2,42,128,512]{3,2,1,0:T(8,128)(2,1)} %param.22), kind=kLoop, calls=%fused_computation.147 | loop fusion | bytes 22020096 | tf_op jit(solution)/shard_map/slice | solution.py:122
  26.4 9.7 %fusion.78 = (bf16[1,42,128,512]{3,2,1,0:T(8,128)(2,1)}, bf16[1,42,128,512]{3,2,1,0:T(8,128)(2,1)}) fusion(bf16[2,42,128,512]{3,2,1,0:T(8,128)(2,1)} %param.23), kind=kLoop, calls=%fused_computation.148 | loop fusion | bytes 22020096 | tf_op jit(solution)/shard_map/slice | solution.py:123
  37.0 22.6 %all-gather.2.cloned.1.call-done = bf16[1024,2048]{1,0:T(8,128)(2,1)} async-done(((bf16[32,2048]{1,0:T(8,128)(2,1)}), bf16[1024,2048]{1,0:T(8,128)(2,1)}) %all-gather.2.cloned.1.call-update) | async-done | bytes 4194320 | tf_op jit(solution)/shard_map/all_gather | solution.py:110
  59.7 3.5 %gather_fusion = bf16[32,2048]{1,0:T(8,128)(2,1)S(1)} fusion(bf16[1024,2048]{1,0:T(8,128)(2,1)} %all-gather.2.cloned.1.call-done, s32[1024]{0:T(1024)S(1)} %pad_clamp_fusion.1), kind=kCustom, calls=%fused_computation.clone | custom fusion | bytes 262272 | tf_op jit(solution)/shard_map/jit(_take)/gather | solution.py:111
  63.2 4.9 %convolution_convert_fusion.1 = bf16[32,1536]{1,0:T(8,128)(2,1)S(1)} fusion(bf16[2048,1536]{0,1:T(8,128)(2,1)} %bitcast.45, bf16[32,2048]{1,0:T(8,128)(2,1)S(1)} %gather_fusion, pred[32]{0:T(512)(128)(4,1)S(1)} %get-tuple-element.8), kind=kOutput, calls=%fused_computation.14 | convolution fusion | flops 201441280 | bytes 6520864 | tf_op jit(solution)/shard_map/dot_general | solution.py:116
  68.3 2.0 fusion.81
  72.1 1.1 convolution_convert_fusion.5
  73.3 38.0 %all-reduce.5.cloned.1.call-done = bf16[32,2048]{1,0:T(8,128)(2,1)} async-done(((bf16[32,2048]{1,0:T(8,128)(2,1)}), bf16[32,2048]{1,0:T(8,128)(2,1)}) %all-reduce.5.cloned.1.call-update) | async-done | bytes 131088 | tf_op jit(solution)/shard_map/psum | solution.py:21
  111.3 1.1 fusion.13
  112.5 1.1 multiply_reduce_fusion.3
  113.6 1.1 add_convert_fusion.3
  114.7 5.7 %convolution_convert_fusion.4 = bf16[32,2048]{1,0:T(8,128)(2,1)} fusion(bf16[1024,2048]{1,0:T(8,128)(2,1)} %param.21, bf16[32,2048]{1,0:T(8,128)(2,1)S(1)} %add_convert_fusion.3, bf16[2048,1024]{1,0:T(8,128)(2,1)} %param.20), kind=kOutput, calls=%fused_computation.17 | convolution fusion | flops 268795904 | bytes 8650752 | tf_op jit(solution)/shard_map/dot_general | solution.py:140
  120.7 41.5 %all-reduce.7.cloned.1.call-done = bf16[32,2048]{1,0:T(8,128)(2,1)} async-done(((bf16[32,2048]{1,0:T(8,128)(2,1)}), bf16[32,2048]{1,0:T(8,128)(2,1)}) %all-reduce.7.cloned.1.call-update) | async-done | bytes 131088 | tf_op jit(solution)/shard_map/psum | solution.py:21
  162.2 1.0 fusion.15
  163.3 1.1 multiply_reduce_fusion.2
  165.4 4.9 %convolution_convert_fusion = bf16[32,1536]{1,0:T(8,128)(2,1)S(1)} fusion(bf16[32,2048]{1,0:T(8,128)(2,1)S(1)} %add_convert_fusion.2, bf16[2048,1536]{0,1:T(8,128)(2,1)} %bitcast.46), kind=kOutput, calls=%fused_computation.13 | convolution fusion | flops 201375744 | bytes 6520832 | tf_op jit(solution)/shard_map/dot_general | solution.py:116
  170.5 4.7 %fusion.82 = (f32[32,4]{0,1:T(4,128)S(1)}, f32[32,4,5376]{2,0,1:T(8,128)S(1)}) fusion(bf16[5376,512,1]{1,0,2:T(8,128)(2,1)} %bitcast.47, pred[4,512]{1,0:T(4,128)(4,1)S(1)} %iota_compare_fusion.1, bf16[32,512]{1,0:T(8,128)(2,1)S(1)} %slice.67, pred[32,5376]{1,0:T(8,128)(4,1)S(1)} %fusion.11), kind=kOutput, calls=%fused_computation.152 | convolution fusion | flops 706772864 | bytes 8464896 | tf_op jit(solution)/shard_map/rhf,tf->rht/dot_general | solution.py:75
  175.8 1.0 fusion.9
  176.9 1.1 convolution_convert_fusion.3
  178.1 41.7 %all-reduce.9.cloned.1.call-done = bf16[32,2048]{1,0:T(8,128)(2,1)} async-done(((bf16[32,2048]{1,0:T(8,128)(2,1)}), bf16[32,2048]{1,0:T(8,128)(2,1)}) %all-reduce.9.cloned.1.call-update) | async-done | bytes 131088 | tf_op jit(solution)/shard_map/psum | solution.py:21
  219.7 1.0 fusion.17
  220.8 1.1 multiply_reduce_fusion.1
  222.9 5.7 %convolution_convert_fusion.2 = bf16[32,2048]{1,0:T(8,128)(2,1)} fusion(bf16[1024,2048]{1,0:T(8,128)(2,1)} %param.21, bf16[32,2048]{1,0:T(8,128)(2,1)S(1)} %add_convert_fusion.1, bf16[2048,1024]{1,0:T(8,128)(2,1)} %param.20), kind=kOutput, calls=%fused_computation.15 | convolution fusion | flops 268795904 | bytes 8650752 | tf_op jit(solution)/shard_map/dot_general | solution.py:140
  228.7 41.7 %all-reduce.11.cloned.1.call-done = bf16[32,2048]{1,0:T(8,128)(2,1)} async-done(((bf16[32,2048]{1,0:T(8,128)(2,1)}), bf16[32,2048]{1,0:T(8,128)(2,1)}) %all-reduce.11.cloned.1.call-update) | async-done | bytes 131088 | tf_op jit(solution)/shard_map/psum | solution.py:21
  270.4 1.0 fusion.19
  271.5 1.1 multiply_reduce_fusion
  273.6 2.5 stack.2
  276.1 9.8 %all-to-all-start = ((bf16[32,32,2048]{2,1,0:T(8,128)(2,1)}), bf16[32,32,2048]{2,1,0:T(8,128)(2,1)}, u32[]{:S(2)}, u32[]{:S(2)}) async-start(bf16[32,32,2048]{2,1,0:T(8,128)(2,1)} %stack.2), calls=%async_computation | async-start | bytes 8388608 | tf_op jit(solution)/shard_map/all_to_all | solution.py:148
  285.9 4.3 %scatter_custom_fusion = s32[1024]{0:T(1024)S(1)} fusion(s32[1024]{0:T(1024)S(1)} %compare_select_fusion, s32[1024]{0:T(1024)S(1)} %iota.51, s32[]{:T(128)} %constant.32.clone.1), kind=kCustom, calls=%fused_computation.111 | custom fusion | bytes 4100 | tf_op jit(solution)/shard_map/scatter | solution.py:144
  290.3 47.8 %all-to-all-done = bf16[32,32,2048]{2,1,0:T(8,128)(2,1)} async-done(((bf16[32,32,2048]{2,1,0:T(8,128)(2,1)}), bf16[32,32,2048]{2,1,0:T(8,128)(2,1)}, u32[]{:S(2)}, u32[]{:S(2)}) %all-to-all-start) | async-done | bytes 4194336 | tf_op jit(solution)/shard_map/all_to_all | solution.py:148
  338.1 3.5 %gather_fusion.1 = bf16[32,2048]{1,0:T(8,128)(2,1)S(1)} fusion(bf16[1024,2048]{1,0:T(8,128)(2,1)} %bitcast.14, s32[1024]{0:T(1024)S(1)} %pad_clamp_fusion), kind=kCustom, calls=%fused_computation.1.clone | custom fusion | bytes 262272 | tf_op jit(solution)/shard_map/jit(_take)/gather | solution.py:150
  (80 shorter events, 9.1 us)
Async XLA Ops:
  6.5 65.5 %copy-start = (bf16[512,2048]{1,0:T(8,128)(2,1)S(1)}, bf16[512,2048]{1,0:T(8,128)(2,1)}, u32[]{:S(2)}) copy-start(bf16[512,2048]{1,0:T(8,128)(2,1)} %param.19) | copy-start | bytes 6291460
  6.5 53.1 %all-gather.2.cloned.1.call-start = ((), (), s32[]{:S(2)}) async-start(), calls=%async_computation.1 | async-start | bytes 4325376 | tf_op jit(solution)/shard_map/all_gather | solution.py:110
  7.3 104.1 %all-reduce.5.cloned.1.call-start = ((), (), s32[]{:S(2)}) async-start(), calls=%async_computation.2 | async-start | bytes 262144 | tf_op jit(solution)/shard_map/psum | solution.py:21
  7.3 8.9 %copy-start.4 = (s32[1024]{0:T(1024)S(1)}, s32[1024]{0:T(1024)}, u32[]{:S(2)}) copy-start(s32[1024]{0:T(1024)} %param.15) | copy-start | bytes 12292
  7.3 9.0 %copy-start.6 = (s32[32]{0:T(128)S(1)}, s32[32]{0:T(128)}, u32[]{:S(2)}) copy-start(s32[32]{0:T(128)} %param.17) | copy-start | bytes 388
  7.3 9.1 %copy-start.5 = (s32[32,6]{0,1:T(8,128)S(1)}, s32[32,6]{0,1:T(8,128)}, u32[]{:S(2)}) copy-start(s32[32,6]{0,1:T(8,128)} %param.16) | copy-start | bytes 2308
  63.2 5.1 %copy-start.1 = (bf16[1,42,128,512]{3,2,1,0:T(8,128)(2,1)S(1)}, bf16[1,42,128,512]{3,2,1,0:T(8,128)(2,1)}, u32[]{:S(2)}) copy-start(bf16[1,42,128,512]{3,2,1,0:T(8,128)(2,1)} %get-tuple-element.11) | copy-start | bytes 16515076
  68.1 2.9 slice-start.2
  68.3 2.7 slice-start.3
  71.0 2.3 copy-start.2
  73.2 89.0 %all-reduce.7.cloned.1.call-start = ((), (), s32[]{:S(2)}) async-start(), calls=%async_computation.3 | async-start | bytes 262144 | tf_op jit(solution)/shard_map/psum | solution.py:21
  114.7 6.0 %copy-start.3 = (f32[2,2048]{1,0:T(2,128)S(1)}, f32[2,2048]{1,0:T(2,128)}, u32[]{:S(2)}) copy-start(f32[2,2048]{1,0:T(2,128)} %param.25) | copy-start | bytes 49156
  120.5 99.3 %all-reduce.9.cloned.1.call-start = ((), (), s32[]{:S(2)}) async-start(), calls=%async_computation.4 | async-start | bytes 262144 | tf_op jit(solution)/shard_map/psum | solution.py:21
  165.4 10.4 %slice-start = ((s8[5505024]{0:T(1024)(128)(4,1)}), s8[4194304]{0:T(1024)(128)(4,1)S(1)}, s32[]{:S(2)}) async-start(s8[5505024]{0:T(1024)(128)(4,1)} %bitcast.49), calls=%async_computation.6 | async-start | bytes 8388608
  170.5 5.4 %slice-start.1 = ((s8[5505024]{0:T(1024)(128)(4,1)}), s8[1310720]{0:T(1024)(128)(4,1)S(1)}, s32[]{:S(2)}) async-start(s8[5505024]{0:T(1024)(128)(4,1)} %bitcast.49), calls=%async_computation.7 | async-start | bytes 2621440
  178.0 92.4 %all-reduce.11.cloned.1.call-start = ((), (), s32[]{:S(2)}) async-start(), calls=%async_computation.5 | async-start | bytes 262144 | tf_op jit(solution)/shard_map/psum | solution.py:21
  276.1 62.0 %all-to-all-start = ((bf16[32,32,2048]{2,1,0:T(8,128)(2,1)}), bf16[32,32,2048]{2,1,0:T(8,128)(2,1)}, u32[]{:S(2)}, u32[]{:S(2)}) async-start(bf16[32,32,2048]{2,1,0:T(8,128)(2,1)} %stack.2), calls=%async_computation | async-start | bytes 8388608 | tf_op jit(solution)/shard_map/all_to_all | solution.py:148
Sparse Core Ops, SparseCore 0:
  9.6 50.0 all-gather.1
  73.3 37.9 all-reduce.4
  120.6 41.5 all-reduce.6
  178.1 41.5 all-reduce.8
  228.8 41.5 all-reduce.10
